TPU v7x, 256 devices: a whole 4x4x8 slice. The times are simulated.
256 devices in a mesh: dp: 32 (over y, x, z_lo), tensor: 8 (over z_hi, core).
Axes of the slice: x: 4, y: 4, z: 8 (z_hi: 4, z_lo: 2; z = z_hi * 2 + z_lo), core: 2. Of those that a mesh axis runs over, the one named last changes fastest.
Arguments:
- grad_out: bfloat16 [24576, 4096], P(('dp', 'tensor')), may hold values from -0.15625 to 0.15625
- activations: bfloat16 [24576, 14336], P('dp', 'tensor'), may hold values from -6 to 6
- grad_dither: float32 [24576, 4096], P(('dp', 'tensor')), may hold values from -0.5 to 0.5
- hidden_dither: float32 [32, 14336], P('dp', 'tensor'), may hold values from -0.25 to 0.25
- feature_dither: float32 [32, 4096], P('dp'), may hold values from -0.25 to 0.25
Outputs:
- weight_grad: float32 [4096, 14336], P('dp', 'tensor')
All inputs are finite; a program needn't handle non-finite values.
Results may differ from a plain program's by a relative error of at most 0.014.
Values may be sent and summed in bfloat16 or wider, within the bound.
A program may use at most 128 MiB of HBM per device.

v0:
```python
import jax
import jax.numpy as jnp
from jax import lax
from jax.sharding import PartitionSpec as P

BLOCK = 128
Y_LEVELS = 8
W_LEVELS = 7
ROW_TILE = 512
epsilon = 1e-06


def decode_rows(code_rows, scale_rows):
    row_total = code_rows.shape[0]
    block_count = code_rows.shape[1] // BLOCK
    held = lax.optimization_barrier(code_rows).astype(jnp.float32)
    values = (
        held.reshape(row_total, block_count, BLOCK) * scale_rows.astype(jnp.float32)[:, :, None]
    )
    return values.reshape(row_total, block_count * BLOCK).astype(jnp.bfloat16)


def decode_terms(code_block, block_scale):
    feat_rows, unit_cols = code_block.shape
    block_count = feat_rows // BLOCK
    held = lax.optimization_barrier(code_block).astype(jnp.float32)
    values = (
        held.reshape(block_count, BLOCK, unit_cols) * block_scale.astype(jnp.float32)[:, None, :]
    )
    return values.reshape(feat_rows, unit_cols).astype(jnp.bfloat16)


def quantize(partial_value, feature_part, hidden_part):
    feat_rows, unit_cols = partial_value.shape
    block_count = feat_rows // BLOCK
    blocks = partial_value.reshape(block_count, BLOCK, unit_cols)
    magnitude = jnp.max(jnp.abs(blocks), axis=1)
    block_scale = ((magnitude + epsilon) / W_LEVELS).astype(jnp.bfloat16)
    scaled = (blocks / block_scale.astype(jnp.float32)[:, None, :]).reshape(feat_rows, unit_cols)
    code_block = (scaled + hidden_part[None, :] + feature_part[:, None]).astype(jnp.bfloat16)
    return (code_block, block_scale)


def per_device(grad_out, activations, grad_dither, hidden_dither, feature_dither):
    row_count, feat_width = grad_out.shape
    block_count = feat_width // BLOCK
    grad_float = grad_out.astype(jnp.float32)
    magnitude = jnp.max(jnp.abs(grad_float).reshape(row_count, block_count, BLOCK), axis=2)
    y_scale = ((magnitude + epsilon) / Y_LEVELS).astype(jnp.bfloat16)
    scaled = (
        grad_float.reshape(row_count, block_count, BLOCK) / y_scale.astype(jnp.float32)[:, :, None]
    )
    y_code = (scaled.reshape(row_count, feat_width) + grad_dither).astype(jnp.bfloat16)
    code_rows, scale_rows = (
        lax.all_gather(y_code, "tensor", axis=0, tiled=True),
        lax.all_gather(y_scale, "tensor", axis=0, tiled=True),
    )
    y_hat = decode_rows(code_rows, scale_rows)
    unit_count = activations.shape[1]
    owners = lax.axis_size("dp")
    own_rows = feat_width // owners
    hidden_noise = hidden_dither[0]
    feature_noise = feature_dither[0]

    def feature_tile(tile_start):
        feat_cols = lax.dynamic_slice_in_dim(y_hat, tile_start, ROW_TILE, 1)
        partial_value = lax.dot_general(
            feat_cols, activations, (((0,), (0,)), ((), ())), preferred_element_type=jnp.float32
        )
        feature_part = lax.dynamic_slice_in_dim(feature_noise, tile_start, ROW_TILE, 0)
        return quantize(partial_value, feature_part, hidden_noise)

    tile_starts = jnp.arange(feat_width // ROW_TILE, dtype=jnp.int32) * ROW_TILE
    code_tiles, scale_tiles = lax.map(feature_tile, tile_starts)
    all_codes = code_tiles.reshape(feat_width, unit_count)
    all_scales = scale_tiles.reshape(block_count, unit_count)
    code_part = lax.all_to_all(all_codes, "dp", split_axis=0, concat_axis=0, tiled=True)
    scale_part = lax.all_to_all(all_scales, "dp", split_axis=0, concat_axis=0, tiled=True)
    unit_cols = code_part.shape[1]
    terms = decode_terms(code_part, scale_part)
    held = lax.optimization_barrier(terms).astype(jnp.float32).reshape(owners, own_rows, unit_cols)
    return jnp.sum(held, axis=0)


def solution(mesh):
    placed = (
        P(("dp", "tensor"), None),
        P("dp", "tensor"),
        P(("dp", "tensor"), None),
        P("dp", "tensor"),
        P("dp", None),
    )
    return jax.shard_map(
        per_device, mesh=mesh, in_specs=placed, out_specs=P("dp", "tensor"), check_vma=False
    )
```

profile of v0, /device:TPU:46, one launch (start us, length us, event | category | flops | bytes accessed | tf_op | source)
XLA Modules:
  0.0 479.5 jit_solution(6907904781474757774)
XLA Ops:
  6.5 0.0 copy-start.1
  6.5 0.0 all-gather.3.cloned.1.call-start
  6.5 1.4 fusion.9
  7.9 0.3 copy.18
  8.2 0.5 reduce_max.18
  8.7 0.5 div.33
  9.2 0.0 copy-done.1
  9.2 3.4 fusion.11
  12.6 0.0 all-gather.3.cloned.1.call-update
  12.6 0.1 copy.11
  12.7 17.3 %all-gather = bf16[8,96,32]{1,2,0:T(8,128)(2,1)S(1)} all-gather(bf16[1,96,32]{1,2,0:T(8,128)(2,1)S(1)} %copy.11), channel_id=1, replica_groups=mesh['dp'=32,'tensor'=8] {'tensor'}, dimensions={0}, use_global_device_ids=true | all-gather | bytes 55296 | tf_op jit(solution)/shard_map/all_gather | solution.py:56
  30.0 0.1 copy.15
  30.1 54.8 %all-gather.3.cloned.1.call-done = bf16[768,4096]{1,0:T(8,128)(2,1)} async-done(((bf16[96,4096]{1,0:T(8,128)(2,1)}), bf16[768,4096]{1,0:T(8,128)(2,1)}) %all-gather.3.cloned.1.call-update) | async-done | bytes 6291472 | tf_op jit(solution)/shard_map/all_gather | solution.py:55
  84.9 7.1 %mul.31 = f32[768,32,128]{2,1,0:T(8,128)} broadcast(f32[768,32]{1,0:T(8,128)S(1)} %bitcast.57), dimensions={0,1} | broadcast | bytes 12681216 | tf_op jit(solution)/shard_map/mul | solution.py:18
  92.0 0.0 copy-start
  92.0 0.0 copy-start.2
  92.0 16.8 %fusion.8 = bf16[768,4096]{1,0:T(8,128)(2,1)} fusion(f32[96,8,32,128]{3,2,1,0:T(8,128)} %bitcast.53, bf16[768,4096]{1,0:T(8,128)(2,1)} %all-gather.3.cloned.1.call-done), kind=kLoop, calls=%fused_computation.16 | loop fusion | flops 9437184 | bytes 25165824 | tf_op jit(solution)/shard_map/convert_element_type | solution.py:20
  108.9 0.0 copy-done
  108.9 0.0 copy-done.2
  108.9 65.0 %while.12 = (s32[]{:T(128)}, bf16[8,512,1792]{2,1,0:T(8,128)(2,1)}, bf16[8,4,1792]{2,1,0:T(4,128)(2,1)S(1)}, s32[8]{0:T(128)S(1)}, bf16[768,4096]{1,0:T(8,128)(2...) while((s32[]{:T(128)}, bf16[8,512,1792]{2,1,0:T(8,128)(2,1)}, ...), condition=%wide.region_3.4_spmd, body=%wide.region_1.3_spmd.sunk | while | flops 1414834176 | bytes 12899519 | solution.py:74
  108.9 0.6 dynamic_slice.18
  111.4 0.8 dynamic_slice.19
  112.2 3.0 bitcast_reduce_fusion.2
  115.3 1.7 bitcast_dynamic-update-slice_fusion.4
  117.0 0.6 dynamic_slice.18
  119.5 0.8 dynamic_slice.19
  120.3 3.0 bitcast_reduce_fusion.2
  123.4 1.7 bitcast_dynamic-update-slice_fusion.4
  125.1 0.6 dynamic_slice.18
  127.6 0.8 dynamic_slice.19
  128.4 3.0 bitcast_reduce_fusion.2
  131.5 1.7 bitcast_dynamic-update-slice_fusion.4
  133.2 0.6 dynamic_slice.18
  135.8 0.8 dynamic_slice.19
  136.6 3.0 bitcast_reduce_fusion.2
  139.6 1.8 bitcast_dynamic-update-slice_fusion.4
  141.4 0.6 dynamic_slice.18
  143.9 0.8 dynamic_slice.19
  144.7 3.0 bitcast_reduce_fusion.2
  147.8 1.8 bitcast_dynamic-update-slice_fusion.4
  149.6 0.6 dynamic_slice.18
  152.1 0.8 dynamic_slice.19
  152.9 3.0 bitcast_reduce_fusion.2
  156.0 1.7 bitcast_dynamic-update-slice_fusion.4
  157.7 0.6 dynamic_slice.18
  160.2 0.8 dynamic_slice.19
  161.0 3.0 bitcast_reduce_fusion.2
  164.1 1.7 bitcast_dynamic-update-slice_fusion.4
  165.8 0.6 dynamic_slice.18
  168.3 0.8 dynamic_slice.19
  169.1 2.9 bitcast_reduce_fusion.2
  172.1 1.7 bitcast_dynamic-update-slice_fusion.4
  173.9 0.1 all_to_all.19
  173.9 0.5 broadcast.64
  174.4 1.3 reduce.1
  175.8 13.3 %all_to_all.22 = bf16[32,2,896]{2,1,0:T(2,128)(2,1)S(1)} all-to-all(bf16[32,2,896]{2,1,0:T(2,128)(2,1)S(1)} %reshape.72), channel_id=1, replica_groups=mesh['dp'=32,'tensor'=8] {'dp'}, dimensions={0} | all-to-all | bytes 229376 | tf_op jit(solution)/shard_map/all_to_all | solution.py:78
  189.1 8.4 %all-to-all-start = ((bf16[32,128,1792]{2,1,0:T(8,128)(2,1)}), bf16[32,128,1792]{2,1,0:T(8,128)(2,1)}, u32[]{:S(2)}, u32[]{:S(2)}) async-start(bf16[32,128,1792]{2,1,0:T(8,128)(2,1)} %bitcast.54), calls=%async_computation | async-start | bytes 29360128 | tf_op jit(solution)/shard_map/all_to_all | solution.py:77
  197.5 0.1 reshape.73
  197.7 252.4 %all-to-all-done = bf16[32,128,1792]{2,1,0:T(8,128)(2,1)} async-done(((bf16[32,128,1792]{2,1,0:T(8,128)(2,1)}), bf16[32,128,1792]{2,1,0:T(8,128)(2,1)}, u32[]{:S(2)}, u32[]{:S(2)}) %all-to-all-start) | async-done | bytes 14680096 | tf_op jit(solution)/shard_map/all_to_all | solution.py:77
  450.1 14.1 %fusion.7 = bf16[4096,1792]{1,0:T(8,128)(2,1)} fusion(bf16[4096,1792]{1,0:T(8,128)(2,1)} %bitcast.9, f32[32,1792]{1,0:T(8,128)S(1)} %bitcast.58), kind=kLoop, calls=%fused_computation.14 | loop fusion | flops 22020096 | bytes 29589504 | tf_op jit(solution)/shard_map/convert_element_type | solution.py:30
  464.2 8.5 %convert_reduce_fusion = f32[128,1792]{1,0:T(8,128)} fusion(bf16[32,128,1792]{2,1,0:T(8,128)(2,1)} %bitcast.52), kind=kLoop, calls=%fused_computation.12 | loop fusion | flops 14450688 | bytes 15597568 | tf_op jit(solution)/shard_map/reduce_sum | solution.py:82
  (30 shorter events, 0.6 us)
Async XLA Ops:
  6.5 2.6 copy-start.1
  6.5 78.4 %all-gather.3.cloned.1.call-start = ((), (), s32[]{:S(2)}) async-start(), calls=%async_computation.2 | async-start | bytes 7077888 | tf_op jit(solution)/shard_map/all_gather | solution.py:55
  92.0 16.8 %copy-start = (bf16[768,1792]{1,0:T(8,128)(2,1)S(1)}, bf16[768,1792]{1,0:T(8,128)(2,1)}, u32[]{:S(2)}) copy-start(bf16[768,1792]{1,0:T(8,128)(2,1)} %param.8) | copy-start | bytes 8257540
  92.0 16.8 %copy-start.2 = (f32[1,1792]{1,0:T(1,128)S(1)}, f32[1,1792]{1,0:T(1,128)}, u32[]{:S(2)}) copy-start(f32[1,1792]{1,0:T(1,128)} %param.10) | copy-start | bytes 21508
  189.1 261.0 %all-to-all-start = ((bf16[32,128,1792]{2,1,0:T(8,128)(2,1)}), bf16[32,128,1792]{2,1,0:T(8,128)(2,1)}, u32[]{:S(2)}, u32[]{:S(2)}) async-start(bf16[32,128,1792]{2,1,0:T(8,128)(2,1)} %bitcast.54), calls=%async_computation | async-start | bytes 29360128 | tf_op jit(solution)/shard_map/all_to_all | solution.py:77
Sparse Core Ops, SparseCore 0:
  12.7 72.1 all-gather.2
where the time goes:
time: 481 us; the launch traced here: 480 us
  waiting for transfers between devices  307 us (64%)
  other arithmetic  60.4 us (13%)
  blocking collectives  30.6 us (6%)
  matrix products  23.9 us (5%)
  local copies, waits for them, and re-layouts  19.7 us (4%)
  loops' own time  15.7 us (3%)
  between operations  13.5 us (3%)
  starting transfers between devices  8.43 us (2%)
    all_to_all x1, waiting for transfers between devices, per_device(): lax.all_to_all(all_codes, 'dp', split_axis=0, concat_axis=0, tiled=True)  252 us
    all_gather x1, waiting for transfers between devices, per_device(): lax.all_gather(y_code, 'tensor', axis=0, tiled=True)  54.8 us
    dot_general x8, matrix products, feature_tile(): lax.dot_general(feat_cols, activations, (((0,), (0,)), ((), ())), preferr...  23.9 us
    all_gather x1, blocking collectives, per_device(): lax.all_gather(y_scale, 'tensor', axis=0, tiled=True)  17.3 us
    convert_element_type x1, other arithmetic, decode_rows(): return values.reshape(row_total, block_count * BLOCK).astype(jnp.bfloat16)  16.8 us
    another operation x1, loops' own time, per_device(): code_tiles, scale_tiles = lax.map(feature_tile, tile_starts)  15.7 us
    dynamic_update_slice x16, other arithmetic, per_device(): code_tiles, scale_tiles = lax.map(feature_tile, tile_starts)  14.2 us
    convert_element_type x1, other arithmetic, decode_terms(): return values.reshape(feat_rows, unit_cols).astype(jnp.bfloat16)  14.1 us
  transfers between devices with their start and end apart: 2, of which 2 were waited for; matrix products, arithmetic and copies ran while one was open for 0% of the time, Pallas kernels for 0%

commit v1 on v0

--- a/solution.py
+++ b/solution.py
@@ -51,8 +51,15 @@
         grad_float.reshape(row_count, block_count, BLOCK) / y_scale.astype(jnp.float32)[:, :, None]
     )
     y_code = (scaled.reshape(row_count, feat_width) + grad_dither).astype(jnp.bfloat16)
+
+    def circles_write(arr, where_dim):
+        z_new = jnp.stack([arr for _ in range(lax.axis_size("tensor"))])
+        current_block = lax.all_to_all(z_new, axis_name="tensor", split_axis=0, concat_axis=0)
+        n_now = jnp.concatenate(current_block, where_dim)
+        return n_now
+
     code_rows, scale_rows = (
-        lax.all_gather(y_code, "tensor", axis=0, tiled=True),
+        circles_write(y_code, 0),
         lax.all_gather(y_scale, "tensor", axis=0, tiled=True),
     )
     y_hat = decode_rows(code_rows, scale_rows)

time: 481 us -> 553 us (1.15)
  blocking collectives: 30.6 us -> 161 us
  waiting for transfers between devices: 307 us -> 252 us
  between operations: 13.5 us -> 0.11 us
  starting transfers between devices: 8.43 us -> 16 us
    all_gather x1, blocking collectives: 17.3 us -> 147 us  [per_device(): lax.all_gather(y_scale, 'tensor', axis=0, tiled=True)]
    all_gather x1 -> x0, waiting for transfers between devices: 54.8 us -> none  [per_device(): lax.all_gather(y_code, 'tensor', axis=0, tiled=True)]
    all_to_all x0 -> x1, starting transfers between devices: none -> 7.57 us  [circles_write(): lax.all_to_all(z_new, axis_name='tensor', split_axis=0, concat_axis=0)]
  transfers between devices with their start and end apart: 2 -> 2, of which waited for: 2 -> 1; matrix products, arithmetic and copies ran while one was open for 0% -> 0% of each run, Pallas kernels for 0% -> 0%
where the time goes in v1:
time: 553 us; the launch traced here: 552 us
  waiting for transfers between devices  252 us (46%)
  blocking collectives  161 us (29%)
  other arithmetic  59.5 us (11%)
  matrix products  23.9 us (4%)
  local copies, waits for them, and re-layouts  23.7 us (4%)
  starting transfers between devices  16 us (3%)
  loops' own time  15.4 us (3%)
    all_to_all x1, waiting for transfers between devices, per_device(): lax.all_to_all(all_codes, 'dp', split_axis=0, concat_axis=0, tiled=True)  252 us
    all_gather x1, blocking collectives, per_device(): lax.all_gather(y_scale, 'tensor', axis=0, tiled=True)  147 us
    dot_general x8, matrix products, feature_tile(): lax.dot_general(feat_cols, activations, (((0,), (0,)), ((), ())), preferr...  23.9 us
    convert_element_type x1, other arithmetic, decode_rows(): return values.reshape(row_total, block_count * BLOCK).astype(jnp.bfloat16)  16.8 us
    another operation x1, loops' own time, per_device(): code_tiles, scale_tiles = lax.map(feature_tile, tile_starts)  15.4 us
    dynamic_update_slice x16, other arithmetic, per_device(): code_tiles, scale_tiles = lax.map(feature_tile, tile_starts)  14.2 us
    convert_element_type x1, other arithmetic, decode_terms(): return values.reshape(feat_rows, unit_cols).astype(jnp.bfloat16)  14.1 us
    all_to_all x1, blocking collectives, per_device(): lax.all_to_all(all_scales, 'dp', split_axis=0, concat_axis=0, tiled=True)  13.8 us
  transfers between devices with their start and end apart: 2, of which 1 were waited for; matrix products, arithmetic and copies ran while one was open for 0% of the time, Pallas kernels for 0%

profile of v1, /device:TPU:46, one launch (start us, length us, event | category | flops | bytes accessed | tf_op | source)
XLA Modules:
  0.0 551.6 jit_solution(15644811520205131575)
XLA Ops:
  0.0 0.0 copy-start.1
  0.0 1.4 fusion.9
  1.4 0.3 copy.18
  1.7 0.5 reduce_max.18
  2.2 0.5 div.33
  2.6 0.0 copy-done.1
  2.6 2.5 fusion.11
  5.2 3.3 stack.2
  8.5 7.6 %all-to-all-start = ((bf16[8,96,4096]{2,1,0:T(8,128)(2,1)}), bf16[8,96,4096]{2,1,0:T(8,128)(2,1)}, u32[]{:S(2)}, u32[]{:S(2)}) async-start(bf16[8,96,4096]{2,1,0:T(8,128)(2,1)} %stack.2), calls=%async_computation | async-start | bytes 12582912 | tf_op jit(solution)/shard_map/all_to_all | solution.py:57
  16.1 0.1 copy.11
  16.2 147.3 %all-gather = bf16[8,96,32]{1,2,0:T(8,128)(2,1)S(1)} all-gather(bf16[1,96,32]{1,2,0:T(8,128)(2,1)S(1)} %copy.11), channel_id=1, replica_groups=mesh['dp'=32,'tensor'=8] {'tensor'}, dimensions={0}, use_global_device_ids=true | all-gather | bytes 55296 | tf_op jit(solution)/shard_map/all_gather | solution.py:63
  163.5 0.1 copy.15
  163.6 0.0 all-to-all-done
  163.6 7.3 %mul.31 = f32[768,32,128]{2,1,0:T(8,128)} broadcast(f32[768,32]{1,0:T(8,128)S(1)} %bitcast.58), dimensions={0,1} | broadcast | bytes 12681216 | tf_op jit(solution)/shard_map/mul | solution.py:18
  171.0 0.0 copy-start
  171.0 0.0 copy-start.2
  171.0 16.8 %fusion.8 = bf16[768,4096]{1,0:T(8,128)(2,1)} fusion(f32[96,8,32,128]{3,2,1,0:T(8,128)} %bitcast.54, bf16[768,4096]{1,0:T(8,128)(2,1)} %bitcast.5), kind=kLoop, calls=%fused_computation.16 | loop fusion | flops 9437184 | bytes 25165824 | tf_op jit(solution)/shard_map/convert_element_type | solution.py:20
  187.8 0.0 copy-done
  187.8 0.0 copy-done.2
  187.8 65.1 %while.12 = (s32[]{:T(128)}, bf16[8,512,1792]{2,1,0:T(8,128)(2,1)}, bf16[8,4,1792]{2,1,0:T(4,128)(2,1)S(1)}, s32[8]{0:T(128)S(1)}, bf16[768,4096]{1,0:T(8,128)(2...) while((s32[]{:T(128)}, bf16[8,512,1792]{2,1,0:T(8,128)(2,1)}, ...), condition=%wide.region_3.4_spmd, body=%wide.region_1.3_spmd.sunk | while | flops 1414834176 | bytes 12899519 | solution.py:81
  187.8 0.6 dynamic_slice.18
  190.4 0.8 dynamic_slice.19
  191.2 3.0 bitcast_reduce_fusion.2
  194.2 1.7 bitcast_dynamic-update-slice_fusion.4
  196.0 0.6 dynamic_slice.18
  198.5 0.8 dynamic_slice.19
  199.3 3.0 bitcast_reduce_fusion.2
  202.4 1.7 bitcast_dynamic-update-slice_fusion.4
  204.1 0.6 dynamic_slice.18
  206.6 0.8 dynamic_slice.19
  207.4 3.0 bitcast_reduce_fusion.2
  210.5 1.7 bitcast_dynamic-update-slice_fusion.4
  212.2 0.6 dynamic_slice.18
  214.8 0.8 dynamic_slice.19
  215.6 3.0 bitcast_reduce_fusion.2
  218.6 1.8 bitcast_dynamic-update-slice_fusion.4
  220.4 0.6 dynamic_slice.18
  223.0 0.8 dynamic_slice.19
  223.8 3.0 bitcast_reduce_fusion.2
  226.8 1.8 bitcast_dynamic-update-slice_fusion.4
  228.6 0.6 dynamic_slice.18
  231.2 0.8 dynamic_slice.19
  232.0 3.0 bitcast_reduce_fusion.2
  235.0 1.7 bitcast_dynamic-update-slice_fusion.4
  236.8 0.6 dynamic_slice.18
  239.3 0.8 dynamic_slice.19
  240.1 3.0 bitcast_reduce_fusion.2
  243.2 1.7 bitcast_dynamic-update-slice_fusion.4
  244.9 0.6 dynamic_slice.18
  247.4 0.8 dynamic_slice.19
  248.2 2.9 bitcast_reduce_fusion.2
  251.2 1.7 bitcast_dynamic-update-slice_fusion.4
  253.0 0.1 all_to_all.23
  253.0 0.5 broadcast.66
  253.5 1.3 reduce.1
  254.9 13.8 %all_to_all.27 = bf16[32,2,896]{2,1,0:T(2,128)(2,1)S(1)} all-to-all(bf16[32,2,896]{2,1,0:T(2,128)(2,1)S(1)} %reshape.78), channel_id=1, replica_groups=mesh['dp'=32,'tensor'=8] {'dp'}, dimensions={0} | all-to-all | bytes 229376 | tf_op jit(solution)/shard_map/all_to_all | solution.py:85
  268.7 8.4 %all-to-all-start.1 = ((bf16[32,128,1792]{2,1,0:T(8,128)(2,1)}), bf16[32,128,1792]{2,1,0:T(8,128)(2,1)}, u32[]{:S(2)}, u32[]{:S(2)}) async-start(bf16[32,128,1792]{2,1,0:T(8,128)(2,1)} %bitcast.55), calls=%async_computation.1 | async-start | bytes 29360128 | tf_op jit(solution)/shard_map/all_to_all | solution.py:84
  277.1 0.1 reshape.79
  277.3 251.7 %all-to-all-done.1 = bf16[32,128,1792]{2,1,0:T(8,128)(2,1)} async-done(((bf16[32,128,1792]{2,1,0:T(8,128)(2,1)}), bf16[32,128,1792]{2,1,0:T(8,128)(2,1)}, u32[]{:S(2)}, u32[]{:S(2)}) %all-to-all-start.1) | async-done | bytes 14680096 | tf_op jit(solution)/shard_map/all_to_all | solution.py:84
  529.0 14.1 %fusion.7 = bf16[4096,1792]{1,0:T(8,128)(2,1)} fusion(bf16[4096,1792]{1,0:T(8,128)(2,1)} %bitcast.10, f32[32,1792]{1,0:T(8,128)S(1)} %bitcast.59), kind=kLoop, calls=%fused_computation.14 | loop fusion | flops 22020096 | bytes 29589504 | tf_op jit(solution)/shard_map/convert_element_type | solution.py:30
  543.1 8.5 %convert_reduce_fusion = f32[128,1792]{1,0:T(8,128)} fusion(bf16[32,128,1792]{2,1,0:T(8,128)(2,1)} %bitcast.53), kind=kLoop, calls=%fused_computation.12 | loop fusion | flops 14450688 | bytes 15597568 | tf_op jit(solution)/shard_map/reduce_sum | solution.py:89
  (30 shorter events, 0.6 us)
Async XLA Ops:
  0.0 2.6 copy-start.1
  8.5 155.1 %all-to-all-start = ((bf16[8,96,4096]{2,1,0:T(8,128)(2,1)}), bf16[8,96,4096]{2,1,0:T(8,128)(2,1)}, u32[]{:S(2)}, u32[]{:S(2)}) async-start(bf16[8,96,4096]{2,1,0:T(8,128)(2,1)} %stack.2), calls=%async_computation | async-start | bytes 12582912 | tf_op jit(solution)/shard_map/all_to_all | solution.py:57
  171.0 16.8 %copy-start = (bf16[768,1792]{1,0:T(8,128)(2,1)S(1)}, bf16[768,1792]{1,0:T(8,128)(2,1)}, u32[]{:S(2)}) copy-start(bf16[768,1792]{1,0:T(8,128)(2,1)} %param.8) | copy-start | bytes 8257540
  171.0 16.8 %copy-start.2 = (f32[1,1792]{1,0:T(1,128)S(1)}, f32[1,1792]{1,0:T(1,128)}, u32[]{:S(2)}) copy-start(f32[1,1792]{1,0:T(1,128)} %param.10) | copy-start | bytes 21508
  268.7 260.3 %all-to-all-start.1 = ((bf16[32,128,1792]{2,1,0:T(8,128)(2,1)}), bf16[32,128,1792]{2,1,0:T(8,128)(2,1)}, u32[]{:S(2)}, u32[]{:S(2)}) async-start(bf16[32,128,1792]{2,1,0:T(8,128)(2,1)} %bitcast.55), calls=%async_computation.1 | async-start | bytes 29360128 | tf_op jit(solution)/shard_map/all_to_all | solution.py:84
